TPU v7x, 512 devices: a whole 4x8x8 slice. The times are simulated.
512 devices in a mesh: ctx: 32 (over z_hi, y, core), tp: 16 (over x, z_lo).
Axes of the slice: x: 4, y: 8, z: 8 (z_hi: 2, z_lo: 4; z = z_hi * 4 + z_lo), core: 2. Of those that a mesh axis runs over, the one named last changes fastest.
Arguments:
- residual: bfloat16 [4352, 8192], P('ctx', 'tp'), may hold values from -64 to 64
- gate_first: bfloat16 [4352, 8192], P('ctx', 'tp'), may hold values from -6 to 6
- gate_second: bfloat16 [4352, 8192], P('ctx', 'tp'), may hold values from -6 to 6
- hyena_value: bfloat16 [4352, 8192], P('ctx', 'tp'), may hold values from -6 to 6
- short_taps: float32 [3, 3, 8192], P(None, None, 'tp'), may hold values from -3.5 to 3.5
- long_taps: bfloat16 [128, 8192], P(None, 'tp'), may hold values from -0.5 to 0.5
- norm_gain: float32 [8192], P('tp'), may hold values from 0.1 to 1.9
- queries: bfloat16 [4352, 8192], P('ctx', 'tp'), may hold values from -8 to 8
- attn_keys: bfloat16 [4352, 8192], P('ctx', 'tp'), may hold values from -8 to 8
Outputs:
- stream: bfloat16 [4352, 8192], P('ctx', 'tp')
- attended: bfloat16 [4352, 8192], P('ctx', 'tp')
All inputs are finite; a program needn't handle non-finite values.
Results may differ from a plain program's by a relative error of at most 0.007.
Values may be sent and summed in bfloat16 or wider, within the bound.
No kernel may reach another device: no remote copies, remote signals or barrier semaphores. Data moves between devices by JAX's collectives and lax.ppermute only.
A program may use at most 64 MiB of HBM per device.

v0:
```python
import math
import jax
import jax.numpy as jnp
from jax import lax
from jax.sharding import PartitionSpec as P

HD = 128


def shifted(value, axis, steps):
    count = lax.axis_size(axis)
    first, last = (max(0, -steps), min(count, count - steps))
    return lax.ppermute(value, axis, [(source, source + steps) for source in range(first, last)])


def featurize(extended, tap_weights, count):
    taps_total = tap_weights.shape[0]
    result = jnp.zeros((count, extended.shape[1]), jnp.float32)
    for lag_index in range(taps_total):
        begin = taps_total - 1 - lag_index
        result = result + tap_weights[lag_index] * extended[begin : begin + count].astype(
            jnp.float32
        )
    return result


def long_filter(extended, long_taps, count):
    filter_len = long_taps.shape[0]
    padded = extended.astype(jnp.float32)
    tap_table = long_taps.astype(jnp.float32)

    def tap_group(group_index, running):
        for inner_index in range(8):
            lag_index = group_index * 8 + inner_index
            window = lax.dynamic_slice_in_dim(padded, filter_len - 1 - lag_index, count, 0)
            running = (
                running + lax.dynamic_index_in_dim(tap_table, lag_index, 0, keepdims=False) * window
            )
        return running

    return lax.fori_loop(
        0, filter_len // 8, tap_group, jnp.zeros((count, extended.shape[1]), jnp.float32)
    )


def shards(
    residual,
    gate_first,
    gate_second,
    hyena_value,
    short_taps,
    long_taps,
    norm_gain,
    queries,
    attn_keys,
):
    rows = residual.shape[0]
    chans = residual.shape[1]
    filter_len = long_taps.shape[0]
    reach = short_taps.shape[1]
    prev_first, prev_second, prev_value = shifted(
        (
            gate_first[rows - reach + 1 :],
            gate_second[rows - reach + 1 :],
            hyena_value[rows - reach + 1 :],
        ),
        "ctx",
        1,
    )
    feat_first = featurize(jnp.concatenate([prev_first, gate_first], axis=0), short_taps[0], rows)
    feat_second = featurize(
        jnp.concatenate([prev_second, gate_second], axis=0), short_taps[1], rows
    )
    feat_value = featurize(jnp.concatenate([prev_value, hyena_value], axis=0), short_taps[2], rows)
    product = (feat_first * feat_value).astype(jnp.bfloat16)
    prev_product = shifted(product[rows - filter_len + 1 :], "ctx", 1)
    extended = jnp.concatenate([prev_product, product], axis=0)
    filtered = long_filter(extended, long_taps, rows)
    stream = (residual.astype(jnp.float32) + feat_second * filtered).astype(jnp.bfloat16)
    stream_f = stream.astype(jnp.float32)
    row_squares = jnp.sum(stream_f * stream_f, axis=1)
    row_totals = lax.psum(row_squares, "tp")
    inverse = 1.0 / jnp.sqrt(row_totals / (chans * lax.axis_size("tp")) + 1e-06)
    heads = chans // HD
    scale = 1.0 / math.sqrt(HD)
    my_index = lax.axis_index("ctx")
    query_pos = my_index * rows + jnp.arange(rows)
    last_query = my_index * rows + rows - 1
    query_heads = queries.reshape(rows, heads, HD)
    init_state = (
        jnp.full((heads, rows), -1e30, jnp.float32),
        jnp.zeros((heads, rows), jnp.float32),
        jnp.zeros((rows, heads, HD), jnp.float32),
    )
    values = (stream_f * inverse[:, None] * norm_gain).astype(jnp.bfloat16)
    key_piece = lax.all_gather(attn_keys, "ctx", axis=0, tiled=True)
    raw_piece = lax.all_gather(values, "ctx", axis=0, tiled=True)
    piece_rows = key_piece.shape[0]
    block = math.gcd(piece_rows, 1536)

    def block_step(block_index, state):
        offset = block_index * block
        key_block = lax.dynamic_slice_in_dim(key_piece, offset, block, 0)
        raw_block = lax.dynamic_slice_in_dim(raw_piece, offset, block, 0)

        def update(current):
            running_max, running_sum, accum = current
            scores = (
                jnp.einsum(
                    "shd,phd->hsp",
                    query_heads,
                    key_block.reshape(block, heads, HD),
                    preferred_element_type=jnp.float32,
                )
                * scale
            )
            key_pos = offset + jnp.arange(block)
            allowed = (key_pos[None, :] <= query_pos[:, None])[None]
            masked = jnp.where(allowed, scores, -1e30)
            new_max = jnp.maximum(running_max, jnp.max(masked, axis=2))
            factor = jnp.exp(running_max - new_max)
            expo = jnp.where(allowed, jnp.exp(scores - new_max[:, :, None]), 0.0)
            new_sum = running_sum * factor + jnp.sum(expo, axis=2)
            weights = expo.astype(jnp.bfloat16)
            contrib = jnp.einsum(
                "hsp,phd->shd",
                weights,
                raw_block.reshape(block, heads, HD),
                preferred_element_type=jnp.float32,
            )
            new_accum = accum * factor.T[:, :, None] + contrib
            return (new_max, new_sum, new_accum)

        def keep_state(current):
            return current

        return lax.cond(offset <= last_query, update, keep_state, state)

    final_state = lax.fori_loop(0, piece_rows // block, block_step, init_state)
    running_sum = final_state[1]
    accum = final_state[2]
    attended = (accum / running_sum.T[:, :, None]).reshape(rows, chans).astype(jnp.bfloat16)
    return (stream, attended)


def solution(mesh):
    placed = (
        P("ctx", "tp"),
        P("ctx", "tp"),
        P("ctx", "tp"),
        P("ctx", "tp"),
        P(None, None, "tp"),
        P(None, "tp"),
        P("tp"),
        P("ctx", "tp"),
        P("ctx", "tp"),
    )
    return jax.shard_map(
        shards,
        mesh=mesh,
        in_specs=placed,
        out_specs=(P("ctx", "tp"), P("ctx", "tp")),
        check_vma=False,
    )
```

profile of v0, /device:TPU:443, one launch (start us, length us, event | category | flops | bytes accessed | tf_op | source)
XLA Modules:
  0.0 276.9 jit_solution(2932315413179396833)
XLA Ops:
  7.2 0.7 all-gather.3.cloned.1.call-update
  8.0 0.7 slice.86
  8.7 1.3 collective-permute-start.1
  10.0 0.7 slice.92
  10.7 1.3 collective-permute-start.2
  11.9 0.9 fusion.26
  12.8 1.7 collective-permute-done.2
  14.5 1.5 multiply_convert_fusion
  16.0 1.3 collective-permute-start.3
  17.3 0.7 slice.80
  18.0 1.3 collective-permute-start
  19.3 0.9 convert_element_type.71
  20.2 0.9 collective-permute-done.3
  21.2 8.7 %while.36 = (s32[]{:T(128)}, f32[136,512]{1,0:T(8,128)S(1)}, f32[128,512]{1,0:T(8,128)S(1)}, f32[263,512]{1,0:T(8,128)S(1)}, s32[]{:T(128)}, /*index=5*/s32[]{:T...) while((s32[]{:T(128)}, f32[136,512]{1,0:T(8,128)S(1)}, ...), condition=%wide.region_1.2_spmd.clone, body=%wide.region_0.1_spmd.clone.sunk | while | flops 1183811 | bytes 2835447 | solution.py:41
  30.1 25.8 %psum.7 = f32[136]{0:T(256)S(1)} all-reduce(f32[136]{0:T(256)S(1)} %get-tuple-element.512), channel_id=1, replica_groups=mesh['ctx'=32,'tp'=16] {'tp'}, use_global_device_ids=true, to_apply=%region_3.4 | all-reduce | flops 136 | bytes 1088 | tf_op jit(solution)/shard_map/psum | solution.py:82
  56.0 0.8 fusion.21
  56.8 58.0 %all-gather.3.cloned.1.call-done = bf16[4352,512]{1,0:T(8,128)(2,1)} async-done(((bf16[136,512]{1,0:T(8,128)(2,1)}), bf16[4352,512]{1,0:T(8,128)(2,1)}) %all-gather.3.cloned.1.call-update) | async-done | bytes 4456464 | tf_op jit(solution)/shard_map/all_gather | solution.py:96
  114.8 6.4 %copy.20 = bf16[4352,512]{0,1:T(8,128)(2,1)} copy(bf16[4352,512]{1,0:T(8,128)(2,1)} %all-gather.3.cloned.1.call-done) | data formatting | bytes 8912896
  121.2 100.1 %all-gather.5.cloned.1.call-done = bf16[4352,512]{1,0:T(8,128)(2,1)} async-done(((bf16[136,512]{1,0:T(8,128)(2,1)}), bf16[4352,512]{1,0:T(8,128)(2,1)}) %all-gather.5.cloned.1.call-update) | async-done | bytes 4456464 | tf_op jit(solution)/shard_map/all_gather | solution.py:97
  221.4 6.6 %copy.22 = bf16[4352,512]{0,1:T(8,128)(2,1)} copy(bf16[4352,512]{1,0:T(8,128)(2,1)} %all-gather.5.cloned.1.call-done) | data formatting | bytes 8912896
  228.0 41.2 %while.35 = (s32[]{:T(128)}, f32[4,136]{1,0:T(4,128)S(1)}, f32[4,136]{1,0:T(4,128)S(1)}, f32[136,4,128]{2,0,1:T(8,128)S(1)}, s32[]{:T(128)}, /*index=5*/bf16[435...) while((s32[]{:T(128)}, f32[4,136]{1,0:T(4,128)S(1)}, ...), condition=%wide.region_9.10_spmd.clone, body=%wide.region_4.9_spmd.clone.sunk | while | flops 72732656 | bytes 4118965 | solution.py:139
  228.0 2.4 conditional.3
  228.0 1.1 constant_dynamic-slice_fusion
  230.4 2.4 conditional.3
  230.5 1.1 constant_dynamic-slice_fusion
  231.6 0.4 select_reduce_fusion
  232.9 2.4 conditional.3
  232.9 1.1 constant_dynamic-slice_fusion
  234.1 0.4 select_reduce_fusion
  235.3 2.4 conditional.3
  235.3 1.1 constant_dynamic-slice_fusion
  236.5 0.4 select_reduce_fusion
  237.7 2.4 conditional.3
  237.7 1.1 constant_dynamic-slice_fusion
  238.9 0.4 select_reduce_fusion
  240.1 2.4 conditional.3
  240.2 1.1 constant_dynamic-slice_fusion
  241.3 0.4 select_reduce_fusion
  242.6 2.4 conditional.3
  242.6 1.1 constant_dynamic-slice_fusion
  243.8 0.4 select_reduce_fusion
  245.0 2.4 conditional.3
  245.0 1.1 constant_dynamic-slice_fusion
  246.2 0.4 select_reduce_fusion
  247.4 2.4 conditional.3
  247.4 1.1 constant_dynamic-slice_fusion
  248.6 0.4 select_reduce_fusion
  249.8 2.4 conditional.3
  249.9 1.1 constant_dynamic-slice_fusion
  252.3 2.4 conditional.3
  252.3 1.1 constant_dynamic-slice_fusion
  254.7 2.4 conditional.3
  254.7 1.1 constant_dynamic-slice_fusion
  257.1 2.4 conditional.3
  257.1 1.1 constant_dynamic-slice_fusion
  259.5 2.4 conditional.3
  259.6 1.1 constant_dynamic-slice_fusion
  262.0 2.4 conditional.3
  262.0 1.1 constant_dynamic-slice_fusion
  264.4 2.4 conditional.3
  264.4 1.1 constant_dynamic-slice_fusion
  266.8 2.4 conditional.3
  266.8 1.1 constant_dynamic-slice_fusion
  269.2 0.8 copy_bitcast_fusion
  (218 shorter events, 24.7 us)
Async XLA Ops:
  7.2 49.6 %copy-start = (bf16[136,512]{1,0:T(8,128)(2,1)S(1)}, bf16[136,512]{1,0:T(8,128)(2,1)}, u32[]{:S(2)}) copy-start(bf16[136,512]{1,0:T(8,128)(2,1)} %param.22) | copy-start | bytes 417796
  7.2 107.6 %all-gather.3.cloned.1.call-start = ((), (), s32[]{:S(2)}) async-start(), calls=%async_computation | async-start | bytes 4595712 | tf_op jit(solution)/shard_map/all_gather | solution.py:96
  7.9 213.5 %all-gather.5.cloned.1.call-start = ((), (), s32[]{:S(2)}) async-start(), calls=%async_computation.1 | async-start | bytes 4595712 | tf_op jit(solution)/shard_map/all_gather | solution.py:97
  8.7 4.2 %collective-permute-start.1 = (bf16[2,512]{1,0:T(2,128)(2,1)S(1)}, bf16[2,512]{1,0:T(2,128)(2,1)S(1)}, u32[]{:S(2)}, u32[]{:S(2)}) collective-permute-start(bf16[2,512]{1,0:T(2,128)(2,1)S(1)} %slice.86), channel_id=1, source_target_pairs={{0,16},{16,32},{32,48},{48,64},{64,80},{80,96},{96,112},{112,128},... | collective-permute-start | bytes 6152 | tf_op jit(solution)/shard_map/ppermute | solution.py:13
  10.7 3.8 %collective-permute-start.2 = (bf16[2,512]{1,0:T(2,128)(2,1)S(1)}, bf16[2,512]{1,0:T(2,128)(2,1)S(1)}, u32[]{:S(2)}, u32[]{:S(2)}) collective-permute-start(bf16[2,512]{1,0:T(2,128)(2,1)S(1)} %slice.92), channel_id=1, source_target_pairs={{0,16},{16,32},{32,48},{48,64},{64,80},{80,96},{96,112},{112,128},... | collective-permute-start | bytes 6152 | tf_op jit(solution)/shard_map/ppermute | solution.py:13
  16.0 5.1 %collective-permute-start.3 = (bf16[127,512]{1,0:T(8,128)(2,1)S(1)}, bf16[127,512]{1,0:T(8,128)(2,1)S(1)}, u32[]{:S(2)}, u32[]{:S(2)}) collective-permute-start(bf16[127,512]{1,0:T(8,128)(2,1)S(1)} %slice.103), channel_id=1, source_target_pairs={{0,16},{16,32},{32,48},{48,64},{64,80},{80,96},{96,112},{112,128},... | collective-permute-start | bytes 390152 | tf_op jit(solution)/shard_map/ppermute | solution.py:13
  18.0 11.9 %collective-permute-start = (bf16[2,512]{1,0:T(2,128)(2,1)S(1)}, bf16[2,512]{1,0:T(2,128)(2,1)S(1)}, u32[]{:S(2)}, u32[]{:S(2)}) collective-permute-start(bf16[2,512]{1,0:T(2,128)(2,1)S(1)} %slice.80), channel_id=1, source_target_pairs={{0,16},{16,32},{32,48},{48,64},{64,80},{80,96},{96,112},{112,128},... | collective-permute-start | bytes 6152 | tf_op jit(solution)/shard_map/ppermute | solution.py:13
  21.2 8.7 %copy-start.2 = (bf16[136,512]{1,0:T(8,128)(2,1)S(1)}, bf16[136,512]{1,0:T(8,128)(2,1)}, u32[]{:S(2)}) copy-start(bf16[136,512]{1,0:T(8,128)(2,1)} %param.17) | copy-start | bytes 417796
  21.2 8.7 %copy-start.3 = (bf16[136,512]{1,0:T(8,128)(2,1)S(1)}, bf16[136,512]{1,0:T(8,128)(2,1)}, u32[]{:S(2)}) copy-start(bf16[136,512]{1,0:T(8,128)(2,1)} %param.15) | copy-start | bytes 417796
  21.2 34.8 %copy-start.4 = (f32[512]{0:T(512)S(1)}, f32[512]{0:T(512)}, u32[]{:S(2)}) copy-start(f32[512]{0:T(512)} %param.21) | copy-start | bytes 6148
  30.1 91.1 %copy-start.1 = (bf16[136,512]{1,0:T(8,128)(2,1)}, bf16[136,512]{1,0:T(8,128)(2,1)S(1)}, u32[]{:S(2)}) copy-start(bf16[136,512]{1,0:T(8,128)(2,1)S(1)} %get-tuple-element.513) | copy-start | bytes 417796
Sparse Core Ops, SparseCore 0:
  11.4 103.3 all-gather.2
  118.8 102.5 all-gather.4
where the time goes:
time: 278 us; the launch traced here: 277 us
  waiting for transfers between devices  161 us (58%)
  local copies, waits for them, and re-layouts  35 us (13%)
  blocking collectives  25.8 us (9%)
  other arithmetic  18.4 us (7%)
  between operations  14.2 us (5%)
  matrix products  12.7 us (5%)
  starting transfers between devices  5.21 us (2%)
  loops' own time  4.14 us (1%)
    all_gather x1, waiting for transfers between devices, shards(): raw_piece = lax.all_gather(values, 'ctx', axis=0, tiled=True)  100 us
    all_gather x1, waiting for transfers between devices, shards(): key_piece = lax.all_gather(attn_keys, 'ctx', axis=0, tiled=True)  58 us
    psum x1, blocking collectives, shards(): row_totals = lax.psum(row_squares, 'tp')  25.8 us
    dynamic_slice x17, local copies, waits for them, and re-layouts, block_step(): raw_block = lax.dynamic_slice_in_dim(raw_piece, offset, block, 0)  18.3 us
    unnamed x13, local copies, waits for them, and re-layouts  13 us
    dot_general x17, matrix products, update(): jnp.einsum('shd,phd->hsp', query_heads, key_block.reshape(block, heads, H...  6.99 us
    reduce_sum x17, other arithmetic, update(): new_sum = running_sum * factor + jnp.sum(expo, axis=2)  6.31 us
    dot_general x17, matrix products, update(): jnp.einsum('hsp,phd->shd', weights, raw_block.reshape(block, heads, HD),...  5.74 us
  transfers between devices with their start and end apart: 6, of which 4 were waited for; matrix products, arithmetic and copies ran while one was open for 7% of the time, Pallas kernels for 0%

commit v1 on v0

--- a/solution.py
+++ b/solution.py
@@ -94,7 +94,15 @@
     )
     values = (stream_f * inverse[:, None] * norm_gain).astype(jnp.bfloat16)
     key_piece = lax.all_gather(attn_keys, "ctx", axis=0, tiled=True)
-    raw_piece = lax.all_gather(values, "ctx", axis=0, tiled=True)
+    raw_piece = jnp.concatenate(
+        lax.all_to_all(
+            jnp.stack(tuple((values for _ in range(lax.psum(1, axis_name="ctx"))))),
+            axis_name="ctx",
+            split_axis=0,
+            concat_axis=0,
+        ),
+        0,
+    )
     piece_rows = key_piece.shape[0]
     block = math.gcd(piece_rows, 1536)
 

time: 278 us -> 297 us (1.068)
  the two profiles are of different devices: /device:TPU:443 before, /device:TPU:319 now
where the time goes in v1:
time: 297 us; the launch traced here: 296 us
  waiting for transfers between devices  146 us (49%)
  local copies, waits for them, and re-layouts  37.3 us (13%)
  starting transfers between devices  33.2 us (11%)
  blocking collectives  30.6 us (10%)
  other arithmetic  17.7 us (6%)
  between operations  14.2 us (5%)
  matrix products  12.7 us (4%)
  loops' own time  4.11 us (1%)
    all_gather x1, waiting for transfers between devices, shards(): key_piece = lax.all_gather(attn_keys, 'ctx', axis=0, tiled=True)  143 us
    psum x1, blocking collectives, shards(): row_totals = lax.psum(row_squares, 'tp')  30.6 us
    all_to_all x1, starting transfers between devices, shards(): lax.all_to_all(jnp.stack(tuple((values for _ in range(lax.psum(1, axis_na...  28.1 us
    dynamic_slice x17, local copies, waits for them, and re-layouts, block_step(): raw_block = lax.dynamic_slice_in_dim(raw_piece, offset, block, 0)  18.3 us
    unnamed x13, local copies, waits for them, and re-layouts  13 us
    dot_general x17, matrix products, update(): jnp.einsum('shd,phd->hsp', query_heads, key_block.reshape(block, heads, H...  6.98 us
    reduce_sum x17, other arithmetic, update(): new_sum = running_sum * factor + jnp.sum(expo, axis=2)  6.31 us
  transfers between devices with their start and end apart: 6, of which 3 were waited for; matrix products, arithmetic and copies ran while one was open for 6% of the time, Pallas kernels for 0%

profile of v1, /device:TPU:319, one launch (start us, length us, event | category | flops | bytes accessed | tf_op | source)
XLA Modules:
  0.0 295.5 jit_solution(7772490203775923589)
XLA Ops:
  7.2 0.7 slice.86
  8.0 1.3 collective-permute-start.1
  9.2 0.7 slice.92
  10.0 1.3 collective-permute-start.2
  11.2 0.9 fusion.26
  12.1 1.7 collective-permute-done.2
  13.8 1.5 multiply_convert_fusion
  15.3 1.3 collective-permute-start.3
  16.6 0.7 slice.80
  17.3 1.3 collective-permute-start
  18.6 0.9 convert_element_type.71
  19.6 0.8 collective-permute-done.3
  20.5 8.7 %while.36 = (s32[]{:T(128)}, f32[136,512]{1,0:T(8,128)S(1)}, f32[128,512]{1,0:T(8,128)S(1)}, f32[263,512]{1,0:T(8,128)S(1)}, s32[]{:T(128)}, /*index=5*/s32[]{:T...) while((s32[]{:T(128)}, f32[136,512]{1,0:T(8,128)S(1)}, ...), condition=%wide.region_1.2_spmd.clone, body=%wide.region_0.1_spmd.clone.sunk | while | flops 1183811 | bytes 2835447 | solution.py:41
  29.4 30.6 %psum.7 = f32[136]{0:T(256)S(1)} all-reduce(f32[136]{0:T(256)S(1)} %get-tuple-element.521), channel_id=1, replica_groups=mesh['ctx'=32,'tp'=16] {'tp'}, use_global_device_ids=true, to_apply=%region_3.4 | all-reduce | flops 136 | bytes 1088 | tf_op jit(solution)/shard_map/psum | solution.py:82
  60.2 2.3 stack.2
  62.5 28.1 %all-to-all-start = ((bf16[32,136,512]{2,1,0:T(8,128)(2,1)}), bf16[32,136,512]{2,1,0:T(8,128)(2,1)}, u32[]{:S(2)}, u32[]{:S(2)}) async-start(bf16[32,136,512]{2,1,0:T(8,128)(2,1)} %stack.2), calls=%async_computation | async-start | bytes 8912896 | tf_op jit(solution)/shard_map/all_to_all | solution.py:98
  90.6 143.1 %all-gather.2.cloned.1.call-done = bf16[4352,512]{1,0:T(8,128)(2,1)} async-done(((bf16[136,512]{1,0:T(8,128)(2,1)}), bf16[4352,512]{1,0:T(8,128)(2,1)}) %all-gather.2.cloned.1.call-update) | async-done | bytes 4456464 | tf_op jit(solution)/shard_map/all_gather | solution.py:96
  233.8 6.5 %copy.26 = bf16[4352,512]{0,1:T(8,128)(2,1)} copy(bf16[4352,512]{1,0:T(8,128)(2,1)} %all-gather.2.cloned.1.call-done) | data formatting | bytes 8912896
  240.3 6.5 %copy.28 = bf16[4352,512]{0,1:T(8,128)(2,1)} copy(bf16[4352,512]{1,0:T(8,128)(2,1)} %bitcast.14) | data formatting | bytes 8912896
  246.8 41.1 %while.35 = (s32[]{:T(128)}, f32[4,136]{1,0:T(4,128)S(1)}, f32[4,136]{1,0:T(4,128)S(1)}, f32[136,4,128]{2,0,1:T(8,128)S(1)}, s32[]{:T(128)}, /*index=5*/bf16[435...) while((s32[]{:T(128)}, f32[4,136]{1,0:T(4,128)S(1)}, ...), condition=%wide.region_9.10_spmd.clone, body=%wide.region_4.9_spmd.clone.sunk | while | flops 72732656 | bytes 4118965 | solution.py:147
  246.8 2.4 conditional.3
  246.8 1.1 constant_dynamic-slice_fusion
  249.2 2.4 conditional.3
  249.2 1.1 constant_dynamic-slice_fusion
  250.4 0.4 select_reduce_fusion
  251.6 2.4 conditional.3
  251.6 1.1 constant_dynamic-slice_fusion
  252.8 0.4 select_reduce_fusion
  254.0 2.4 conditional.3
  254.1 1.1 constant_dynamic-slice_fusion
  255.3 0.4 select_reduce_fusion
  256.5 2.4 conditional.3
  256.5 1.1 constant_dynamic-slice_fusion
  258.9 2.4 conditional.3
  258.9 1.1 constant_dynamic-slice_fusion
  261.3 2.4 conditional.3
  261.3 1.1 constant_dynamic-slice_fusion
  262.5 0.4 select_reduce_fusion
  263.7 2.4 conditional.3
  263.7 1.1 constant_dynamic-slice_fusion
  264.9 0.4 select_reduce_fusion
  266.1 2.4 conditional.3
  266.2 1.1 constant_dynamic-slice_fusion
  267.4 0.4 select_reduce_fusion
  268.6 2.4 conditional.3
  268.6 1.1 constant_dynamic-slice_fusion
  271.0 2.4 conditional.3
  271.0 1.1 constant_dynamic-slice_fusion
  273.4 2.4 conditional.3
  273.4 1.1 constant_dynamic-slice_fusion
  274.6 0.4 select_reduce_fusion
  275.8 2.4 conditional.3
  275.8 1.1 constant_dynamic-slice_fusion
  277.0 0.4 select_reduce_fusion
  278.2 2.4 conditional.3
  278.2 1.1 constant_dynamic-slice_fusion
  279.4 0.4 select_reduce_fusion
  280.6 2.4 conditional.3
  280.7 1.1 constant_dynamic-slice_fusion
  283.1 2.4 conditional.3
  283.1 1.1 constant_dynamic-slice_fusion
  285.5 2.4 conditional.3
  285.5 1.1 constant_dynamic-slice_fusion
  287.9 0.8 copy_bitcast_fusion
  (218 shorter events, 24.3 us)
Async XLA Ops:
  7.2 83.4 %copy-start = (bf16[136,512]{1,0:T(8,128)(2,1)S(1)}, bf16[136,512]{1,0:T(8,128)(2,1)}, u32[]{:S(2)}) copy-start(bf16[136,512]{1,0:T(8,128)(2,1)} %param.22) | copy-start | bytes 417796
  7.2 226.6 %all-gather.2.cloned.1.call-start = ((), (), s32[]{:S(2)}) async-start(), calls=%async_computation.1 | async-start | bytes 4595712 | tf_op jit(solution)/shard_map/all_gather | solution.py:96
  8.0 4.2 %collective-permute-start.1 = (bf16[2,512]{1,0:T(2,128)(2,1)S(1)}, bf16[2,512]{1,0:T(2,128)(2,1)S(1)}, u32[]{:S(2)}, u32[]{:S(2)}) collective-permute-start(bf16[2,512]{1,0:T(2,128)(2,1)S(1)} %slice.86), channel_id=1, source_target_pairs={{0,16},{16,32},{32,48},{48,64},{64,80},{80,96},{96,112},{112,128},... | collective-permute-start | bytes 6152 | tf_op jit(solution)/shard_map/ppermute | solution.py:13
  10.0 3.8 %collective-permute-start.2 = (bf16[2,512]{1,0:T(2,128)(2,1)S(1)}, bf16[2,512]{1,0:T(2,128)(2,1)S(1)}, u32[]{:S(2)}, u32[]{:S(2)}) collective-permute-start(bf16[2,512]{1,0:T(2,128)(2,1)S(1)} %slice.92), channel_id=1, source_target_pairs={{0,16},{16,32},{32,48},{48,64},{64,80},{80,96},{96,112},{112,128},... | collective-permute-start | bytes 6152 | tf_op jit(solution)/shard_map/ppermute | solution.py:13
  15.3 5.1 %collective-permute-start.3 = (bf16[127,512]{1,0:T(8,128)(2,1)S(1)}, bf16[127,512]{1,0:T(8,128)(2,1)S(1)}, u32[]{:S(2)}, u32[]{:S(2)}) collective-permute-start(bf16[127,512]{1,0:T(8,128)(2,1)S(1)} %slice.103), channel_id=1, source_target_pairs={{0,16},{16,32},{32,48},{48,64},{64,80},{80,96},{96,112},{112,128},... | collective-permute-start | bytes 390152 | tf_op jit(solution)/shard_map/ppermute | solution.py:13
  17.3 11.9 %collective-permute-start = (bf16[2,512]{1,0:T(2,128)(2,1)S(1)}, bf16[2,512]{1,0:T(2,128)(2,1)S(1)}, u32[]{:S(2)}, u32[]{:S(2)}) collective-permute-start(bf16[2,512]{1,0:T(2,128)(2,1)S(1)} %slice.80), channel_id=1, source_target_pairs={{0,16},{16,32},{32,48},{48,64},{64,80},{80,96},{96,112},{112,128},... | collective-permute-start | bytes 6152 | tf_op jit(solution)/shard_map/ppermute | solution.py:13
  20.5 8.7 %copy-start.2 = (bf16[136,512]{1,0:T(8,128)(2,1)S(1)}, bf16[136,512]{1,0:T(8,128)(2,1)}, u32[]{:S(2)}) copy-start(bf16[136,512]{1,0:T(8,128)(2,1)} %param.17) | copy-start | bytes 417796
  20.5 8.7 %copy-start.3 = (bf16[136,512]{1,0:T(8,128)(2,1)S(1)}, bf16[136,512]{1,0:T(8,128)(2,1)}, u32[]{:S(2)}) copy-start(bf16[136,512]{1,0:T(8,128)(2,1)} %param.15) | copy-start | bytes 417796
  20.5 39.6 %copy-start.4 = (f32[512]{0:T(512)S(1)}, f32[512]{0:T(512)}, u32[]{:S(2)}) copy-start(f32[512]{0:T(512)} %param.21) | copy-start | bytes 6148
  29.4 33.1 %copy-start.1 = (bf16[136,512]{1,0:T(8,128)(2,1)}, bf16[136,512]{1,0:T(8,128)(2,1)S(1)}, u32[]{:S(2)}) copy-start(bf16[136,512]{1,0:T(8,128)(2,1)S(1)} %get-tuple-element.522) | copy-start | bytes 417796
  62.5 177.8 %all-to-all-start = ((bf16[32,136,512]{2,1,0:T(8,128)(2,1)}), bf16[32,136,512]{2,1,0:T(8,128)(2,1)}, u32[]{:S(2)}, u32[]{:S(2)}) async-start(bf16[32,136,512]{2,1,0:T(8,128)(2,1)} %stack.2), calls=%async_computation | async-start | bytes 8912896 | tf_op jit(solution)/shard_map/all_to_all | solution.py:98
Sparse Core Ops, SparseCore 0:
  18.7 214.9 all-gather.1
